TPU v7x, 256 devices: a whole 4x4x8 slice. The times are simulated.
256 devices in a mesh: side: 2 (over x_lo), grp: 8 (over z), blk: 16 (over y, x_hi, core).
Axes of the slice: x: 4 (x_hi: 2, x_lo: 2; x = x_hi * 2 + x_lo), y: 4, z: 8, core: 2. Of those that a mesh axis runs over, the one named last changes fastest.
Arguments:
- embed_codes: bfloat16 [2, 65536, 128], P('side', ('grp', 'blk')), may hold values from -4 to 4
- embed_exps: int32 [2, 512], P('side', ('grp', 'blk')), may hold values from -1 to 1
- degrees: int32 [2, 65536], P('side', ('grp', 'blk')), may hold values from 16 to 128
- adjacency: bfloat16 [2, 49152, 128, 128], P('side', ('grp', 'blk')), may hold values from 0 to 1
- block_index: int32 [2, 2, 49152], P('side', None, ('grp', 'blk')), may hold values from 0 to 64, as said below
Outputs:
- layer_rows: bfloat16 [2, 65536, 128], P('side', ('grp', 'blk'))
Inputs may be any that keep to these rules, and one draw needn't show every extreme that they name: `block_index`: each device's list of 384 slots: its used slots come first, in non-decreasing source tile (row 1 below 64), with distinct (destination, source) pairs and destination tiles below 32; the remaining slots have source 64 and destination 0. Every list uses 384 // 4 slots or more, and in each section one list uses all 384.
All inputs are finite; a program needn't handle non-finite values.
Results may differ from a plain program's by a relative error of at most 0.0048.
Values may be sent and summed in bfloat16 or wider, within the bound.
A program may use at most 128 MiB of HBM per device.

v0:
```python
import jax
import jax.numpy as jnp
from jax import lax
from jax.sharding import PartitionSpec as P


def swapped(value, axis, stride):
    mask = 2**stride
    pairs = [(source, source ^ mask) for source in range(lax.axis_size(axis))]
    return lax.ppermute(value, axis, pairs)


def scale_rows(codes_part, exps_part, degree_part, tile_rows):
    scale = jnp.repeat(jnp.exp2(exps_part.astype(jnp.float32)), tile_rows, axis=1)
    inverse = lax.rsqrt(degree_part.astype(jnp.float32))
    return (codes_part.astype(jnp.float32) * scale[..., None] * inverse[..., None]).astype(
        jnp.bfloat16
    )


def shards(embed_codes, embed_exps, degrees, adjacency, block_index):
    tile_rows = adjacency.shape[2]
    row_width = embed_codes.shape[2]
    row_count = embed_codes.shape[1]
    tiles_dev = row_count // tile_rows
    groups = lax.axis_size("grp")
    dest_tiles = groups * tiles_dev
    capacity = adjacency.shape[1]
    other_codes, other_exps, other_degrees = swapped((embed_codes, embed_exps, degrees), "side", 0)
    source = scale_rows(other_codes, other_exps, other_degrees, tile_rows)
    panels = source.reshape(tiles_dev, tile_rows, row_width)
    target_tile = block_index[0, 0]
    source_tile = block_index[0, 1]
    own_blocks = adjacency[0]
    starting = jnp.zeros((dest_tiles, tile_rows, row_width), jnp.float32)
    piece = lax.all_gather(panels, "blk", axis=0, tiled=True)
    start = jnp.int32(0)
    piece_tiles = piece.shape[0]
    window = min(piece_tiles * dest_tiles, capacity)
    range_begin = jnp.sum((source_tile < start).astype(jnp.int32))
    range_end = jnp.sum((source_tile < start + piece_tiles).astype(jnp.int32))
    window_start = jnp.minimum(range_begin, capacity - window)
    picked = window_start + jnp.arange(window, dtype=jnp.int32)
    active = (picked >= range_begin) & (picked < range_end)
    offset_tiles = source_tile
    offset_tiles = jnp.clip(offset_tiles, 0, piece_tiles - 1)
    chosen = jnp.take(piece, offset_tiles, axis=0)
    products = jnp.einsum("kij,kjw->kiw", own_blocks, chosen, preferred_element_type=jnp.float32)
    placed = jnp.where(active, target_tile, dest_tiles)
    running = starting.at[placed].add(products, mode="drop")
    summed = lax.psum_scatter(
        running.reshape(groups, row_count, row_width), "grp", scatter_dimension=0, tiled=True
    )
    inverse = lax.rsqrt(degrees.astype(jnp.float32))
    return (summed * inverse[..., None]).astype(jnp.bfloat16)


def solution(mesh):
    placed = (
        P("side", ("grp", "blk"), None),
        P("side", ("grp", "blk")),
        P("side", ("grp", "blk")),
        P("side", ("grp", "blk"), None, None),
        P("side", None, ("grp", "blk")),
    )
    return jax.shard_map(
        shards,
        mesh=mesh,
        in_specs=placed,
        out_specs=P("side", ("grp", "blk"), None),
        check_vma=False,
    )
```

profile of v0, /device:TPU:2, one launch (start us, length us, event | category | flops | bytes accessed | tf_op | source)
XLA Modules:
  0.0 231.5 jit_solution(15946448544255334482)
XLA Ops:
  6.5 0.0 all-gather.2.cloned.1.call-start
  6.5 2.2 collective-permute-start
  8.8 0.0 collective-permute-start.2
  8.8 2.0 collective-permute-start.1
  10.8 1.9 collective-permute-done.1
  12.7 0.1 broadcast_bitcast_fusion
  12.7 0.0 collective-permute-done.2
  12.8 0.0 collective-permute-done
  12.8 0.9 multiply_convert_fusion.1
  13.6 0.0 all-gather.2.cloned.1.call-update
  13.7 0.0 reduce-scatter.2.cloned.1.call-start
  13.7 1.4 clamp_reduce_fusion
  15.7 2.0 fusion.11
  17.7 50.3 %all-gather.2.cloned.1.call-done = bf16[64,128,128]{2,1,0:T(8,128)(2,1)} async-done(((bf16[4,128,128]{2,1,0:T(8,128)(2,1)}), bf16[64,128,128]{2,1,0:T(8,128)(2,1)}) %all-gather.2.cloned.1.call-update) | async-done | bytes 2097168 | tf_op jit(solution)/shard_map/all_gather | solution.py:36
  68.1 12.9 %gather_fusion = bf16[384,128,128]{2,1,0:T(8,128)(2,1)} fusion(bf16[64,128,128]{2,1,0:T(8,128)(2,1)} %all-gather.2.cloned.1.call-done, s32[1024]{0:T(1024)S(1)} %pad_clamp_fusion), kind=kCustom, calls=%fused_computation | custom fusion | bytes 25167360 | tf_op jit(solution)/shard_map/jit(_take)/gather | solution.py:47
  81.0 22.7 %fusion.4 = f32[384,128,128]{1,2,0:T(8,128)} fusion(bf16[1,384,128,128]{3,2,1,0:T(8,128)(2,1)} %param.8, bf16[384,128,128]{2,1,0:T(8,128)(2,1)} %gather_fusion, pred[384]{0:T(512)(128)(4,1)S(1)} %compare_and_fusion), kind=kOutput, calls=%fused_computation.6 | convolution fusion | flops 1616904192 | bytes 50332032 | tf_op jit(solution)/shard_map/kij,kjw->kiw/dot_general | solution.py:48
  103.7 24.7 %copy.10 = f32[384,128,128]{2,1,0:T(8,128)} copy(f32[384,128,128]{1,2,0:T(8,128)} %fusion.4) | data formatting | bytes 50331648 | tf_op jit(solution)/shard_map/kij,kjw->kiw/dot_general | solution.py:48
  128.3 0.2 broadcast_in_dim.25
  128.6 0.0 copy-start.1
  128.6 50.2 %scatter_fusion = f32[32,128,128]{2,1,0:T(8,128)S(1)} fusion(f32[32,128,128]{2,1,0:T(8,128)S(1)} %broadcast_in_dim.25, s32[384]{0:T(512)S(1)} %get-tuple-element.9, f32[384,128,128]{2,1,0:T(8,128)} %copy.10), kind=kCustom, calls=%fused_computation.1 | custom fusion | flops 6291456 | bytes 75499008 | tf_op jit(solution)/shard_map/scatter-add | solution.py:50
  178.8 0.0 copy-start
  178.8 1.3 copy-done
  180.1 0.0 reduce-scatter.2.cloned.1.call-update
  180.2 0.0 copy-done.1
  180.2 42.7 %reduce-scatter.2.cloned.1.call-done = f32[1,512,128]{2,1,0:T(8,128)} async-done(((f32[8,512,128]{2,1,0:T(8,128)}), f32[1,512,128]{2,1,0:T(8,128)}) %reduce-scatter.2.cloned.1.call-update) | async-done | bytes 262160 | tf_op jit(solution)/shard_map/reduce_scatter | solution.py:51
  222.9 1.7 multiply_convert_fusion
  (5 shorter events, 0.0 us)
Async XLA Ops:
  6.5 61.5 %all-gather.2.cloned.1.call-start = ((), (), s32[]{:S(2)}) async-start(), calls=%async_computation.1 | async-start | bytes 2228224 | tf_op jit(solution)/shard_map/all_gather | solution.py:36
  6.5 6.2 %collective-permute-start = (bf16[1,512,128]{2,1,0:T(8,128)(2,1)}, bf16[1,512,128]{2,1,0:T(8,128)(2,1)S(1)}, u32[]{:S(2)}, u32[]{:S(2)}) collective-permute-start(bf16[1,512,128]{2,1,0:T(8,128)(2,1)} %param.5), channel_id=1, source_target_pairs={{0,128},{128,0},{1,129},{129,1},{2,130},{130,2},{3,131},{131,3},{4... | collective-permute-start | bytes 393224 | tf_op jit(solution)/shard_map/ppermute | solution.py:10
  8.8 4.0 %collective-permute-start.2 = (s32[1,512]{1,0:T(1,128)}, s32[1,512]{1,0:T(1,128)S(1)}, u32[]{:S(2)}, u32[]{:S(2)}) collective-permute-start(s32[1,512]{1,0:T(1,128)} %param.7), channel_id=1, source_target_pairs={{0,128},{128,0},{1,129},{129,1},{2,130},{130,2},{3,131},{131,3},{4... | collective-permute-start | bytes 6152 | tf_op jit(solution)/shard_map/ppermute | solution.py:10
  8.8 3.9 %collective-permute-start.1 = (s32[1,4]{1,0:T(1,128)}, s32[1,4]{1,0:T(1,128)S(1)}, u32[]{:S(2)}, u32[]{:S(2)}) collective-permute-start(s32[1,4]{1,0:T(1,128)} %param.6), channel_id=1, source_target_pairs={{0,128},{128,0},{1,129},{129,1},{2,130},{130,2},{3,131},{131,3},{4... | collective-permute-start | bytes 56 | tf_op jit(solution)/shard_map/ppermute | solution.py:10
  13.7 209.2 %reduce-scatter.2.cloned.1.call-start = ((), (), s32[]{:S(2)}) async-start(), calls=%async_computation.2 | async-start | bytes 2359296 | tf_op jit(solution)/shard_map/reduce_scatter | solution.py:51
  128.6 51.6 %copy-start.1 = (s32[1,512]{1,0:T(1,128)S(1)}, s32[1,512]{1,0:T(1,128)}, u32[]{:S(2)}) copy-start(s32[1,512]{1,0:T(1,128)} %param.7) | copy-start | bytes 6148
  178.8 1.4 copy-start
Sparse Core Ops, SparseCore 0:
  13.8 54.2 all-gather.1
  180.3 42.5 reduce-scatter.1
where the time goes:
time: 233 us; the launch traced here: 231 us
  waiting for transfers between devices  95 us (41%)
  other arithmetic  56.2 us (24%)
  local copies, waits for them, and re-layouts  39.2 us (17%)
  matrix products  22.7 us (10%)
  between operations  14.1 us (6%)
  starting transfers between devices  4.31 us (2%)
    all_gather x1, waiting for transfers between devices, shards(): piece = lax.all_gather(panels, 'blk', axis=0, tiled=True)  50.3 us
    scatter-add x1, other arithmetic, shards(): running = starting.at[placed].add(products, mode='drop')  50.2 us
    reduce_scatter x1, waiting for transfers between devices, shards(): lax.psum_scatter(running.reshape(groups, row_count, row_width), 'grp', sc...  42.7 us
    dot_general x1, local copies, waits for them, and re-layouts, shards(): jnp.einsum('kij,kjw->kiw', own_blocks, chosen, preferred_element_type=jnp...  24.7 us
    dot_general x1, matrix products, shards(): jnp.einsum('kij,kjw->kiw', own_blocks, chosen, preferred_element_type=jnp...  22.7 us
    gather x1, local copies, waits for them, and re-layouts, shards(): chosen = jnp.take(piece, offset_tiles, axis=0)  12.9 us
  transfers between devices with their start and end apart: 5, of which 3 were waited for; matrix products, arithmetic and copies ran while one was open for 2% of the time, Pallas kernels for 0%

commit v1 on v0

--- a/solution.py
+++ b/solution.py
@@ -2,6 +2,15 @@
 import jax.numpy as jnp
 from jax import lax
 from jax.sharding import PartitionSpec as P
+
+
+def _update_target(arr_in):
+    stack_in = []
+    for _ in range(lax.axis_size("blk")):
+        stack_in.append(arr_in)
+    w_next = lax.all_to_all(jnp.stack(stack_in), "blk", 0, 0)
+    field_out = jnp.concatenate(w_next, axis=0)
+    return field_out
 
 
 def swapped(value, axis, stride):
@@ -33,7 +42,7 @@
     source_tile = block_index[0, 1]
     own_blocks = adjacency[0]
     starting = jnp.zeros((dest_tiles, tile_rows, row_width), jnp.float32)
-    piece = lax.all_gather(panels, "blk", axis=0, tiled=True)
+    piece = _update_target(panels)
     start = jnp.int32(0)
     piece_tiles = piece.shape[0]
     window = min(piece_tiles * dest_tiles, capacity)

time: 233 us -> 213 us (0.914)
  waiting for transfers between devices: 95 us -> 69.2 us
  starting transfers between devices: 4.31 us -> 10 us
    all_gather x1 -> x0, waiting for transfers between devices: 50.3 us -> none  [shards(): piece = lax.all_gather(panels, 'blk', axis=0, tiled=True)]
    all_to_all x0 -> x1, waiting for transfers between devices: none -> 25.3 us  [_update_target(): w_next = lax.all_to_all(jnp.stack(stack_in), 'blk', 0, 0)]
    all_to_all x0 -> x1, starting transfers between devices: none -> 5.74 us  [_update_target(): w_next = lax.all_to_all(jnp.stack(stack_in), 'blk', 0, 0)]
where the time goes in v1:
time: 213 us; the launch traced here: 211 us
  waiting for transfers between devices  69.2 us (32%)
  other arithmetic  55.6 us (26%)
  local copies, waits for them, and re-layouts  39.5 us (19%)
  matrix products  22.7 us (11%)
  between operations  14.1 us (7%)
  starting transfers between devices  10 us (5%)
    scatter-add x1, other arithmetic, shards(): running = starting.at[placed].add(products, mode='drop')  50.2 us
    reduce_scatter x1, waiting for transfers between devices, shards(): lax.psum_scatter(running.reshape(groups, row_count, row_width), 'grp', sc...  42.1 us
    all_to_all x1, waiting for transfers between devices, _update_target(): w_next = lax.all_to_all(jnp.stack(stack_in), 'blk', 0, 0)  25.3 us
    dot_general x1, local copies, waits for them, and re-layouts, shards(): jnp.einsum('kij,kjw->kiw', own_blocks, chosen, preferred_element_type=jnp...  24.7 us
    dot_general x1, matrix products, shards(): jnp.einsum('kij,kjw->kiw', own_blocks, chosen, preferred_element_type=jnp...  22.7 us
    gather x1, local copies, waits for them, and re-layouts, shards(): chosen = jnp.take(piece, offset_tiles, axis=0)  11.3 us
    all_to_all x1, starting transfers between devices, _update_target(): w_next = lax.all_to_all(jnp.stack(stack_in), 'blk', 0, 0)  5.74 us
    ppermute x3, starting transfers between devices, swapped(): return lax.ppermute(value, axis, pairs)  4.27 us
  transfers between devices with their start and end apart: 5, of which 3 were waited for; matrix products, arithmetic and copies ran while one was open for 2% of the time, Pallas kernels for 0%

profile of v1, /device:TPU:2, one launch (start us, length us, event | category | flops | bytes accessed | tf_op | source)
XLA Modules:
  0.0 211.1 jit_solution(1724848971624185353)
XLA Ops:
  6.5 2.2 %collective-permute-start = (bf16[1,512,128]{2,1,0:T(8,128)(2,1)}, bf16[1,512,128]{2,1,0:T(8,128)(2,1)S(1)}, u32[]{:S(2)}, u32[]{:S(2)}) collective-permute-start(bf16[1,512,128]{2,1,0:T(8,128)(2,1)} %param.5), channel_id=1, source_target_pairs={{0,128},{128,0},{1,129},{129,1},{2,130},{130,2},{3,131},{131,3},{4... | collective-permute-start | bytes 393224 | tf_op jit(solution)/shard_map/ppermute | solution.py:19
  8.8 0.0 collective-permute-start.2
  8.8 2.0 collective-permute-start.1
  10.8 1.9 collective-permute-done.1
  12.7 0.1 broadcast_bitcast_fusion
  12.7 0.0 collective-permute-done.2
  12.8 0.0 collective-permute-done
  12.8 0.2 multiply_convert_fusion.1
  13.0 1.9 stack.3
  14.8 5.7 %all-to-all-start = ((bf16[16,4,128,128]{3,2,1,0:T(8,128)(2,1)}), bf16[16,4,128,128]{3,2,1,0:T(8,128)(2,1)S(1)}, u32[]{:S(2)}, u32[]{:S(2)}) async-start(bf16[16,4,128,128]{3,2,1,0:T(8,128)(2,1)} %stack.3), calls=%async_computation | async-start | bytes 4194304 | tf_op jit(solution)/shard_map/all_to_all | solution.py:11
  20.6 0.0 reduce-scatter.2.cloned.1.call-start
  20.6 1.3 clamp_reduce_fusion
  22.6 2.0 fusion.11
  24.7 25.3 %all-to-all-done = bf16[16,4,128,128]{3,2,1,0:T(8,128)(2,1)S(1)} async-done(((bf16[16,4,128,128]{3,2,1,0:T(8,128)(2,1)}), bf16[16,4,128,128]{3,2,1,0:T(8,128)(2,1)S(1)}, u32[]{:S(2)}, u32[]{:S(2)}) %all-to-all-start) | async-done | bytes 2097184 | tf_op jit(solution)/shard_map/all_to_all | solution.py:11
  50.0 11.3 %gather_fusion = bf16[384,128,128]{2,1,0:T(8,128)(2,1)} fusion(bf16[64,128,128]{2,1,0:T(8,128)(2,1)S(1)} %bitcast.23, s32[1024]{0:T(1024)S(1)} %pad_clamp_fusion), kind=kCustom, calls=%fused_computation | custom fusion | bytes 25167360 | tf_op jit(solution)/shard_map/jit(_take)/gather | solution.py:56
  61.3 22.7 %fusion.4 = f32[384,128,128]{1,2,0:T(8,128)} fusion(bf16[1,384,128,128]{3,2,1,0:T(8,128)(2,1)} %param.8, bf16[384,128,128]{2,1,0:T(8,128)(2,1)} %gather_fusion, pred[384]{0:T(512)(128)(4,1)S(1)} %compare_and_fusion), kind=kOutput, calls=%fused_computation.6 | convolution fusion | flops 1616904192 | bytes 50332032 | tf_op jit(solution)/shard_map/kij,kjw->kiw/dot_general | solution.py:57
  84.0 24.7 %copy.8 = f32[384,128,128]{2,1,0:T(8,128)} copy(f32[384,128,128]{1,2,0:T(8,128)} %fusion.4) | data formatting | bytes 50331648 | tf_op jit(solution)/shard_map/kij,kjw->kiw/dot_general | solution.py:57
  108.6 0.2 broadcast_in_dim.25
  108.9 0.0 copy-start.1
  108.9 50.2 %scatter_fusion = f32[32,128,128]{2,1,0:T(8,128)S(1)} fusion(f32[32,128,128]{2,1,0:T(8,128)S(1)} %broadcast_in_dim.25, s32[384]{0:T(512)S(1)} %get-tuple-element.9, f32[384,128,128]{2,1,0:T(8,128)} %copy.8), kind=kCustom, calls=%fused_computation.1 | custom fusion | flops 6291456 | bytes 75499008 | tf_op jit(solution)/shard_map/scatter-add | solution.py:59
  159.1 0.0 copy-start
  159.1 1.3 copy-done
  160.4 0.0 reduce-scatter.2.cloned.1.call-update
  160.5 0.0 copy-done.1
  160.5 42.1 %reduce-scatter.2.cloned.1.call-done = f32[1,512,128]{2,1,0:T(8,128)} async-done(((f32[8,512,128]{2,1,0:T(8,128)}), f32[1,512,128]{2,1,0:T(8,128)}) %reduce-scatter.2.cloned.1.call-update) | async-done | bytes 262160 | tf_op jit(solution)/shard_map/reduce_scatter | solution.py:60
  202.6 1.7 multiply_convert_fusion
  (5 shorter events, 0.0 us)
Async XLA Ops:
  6.5 6.2 %collective-permute-start = (bf16[1,512,128]{2,1,0:T(8,128)(2,1)}, bf16[1,512,128]{2,1,0:T(8,128)(2,1)S(1)}, u32[]{:S(2)}, u32[]{:S(2)}) collective-permute-start(bf16[1,512,128]{2,1,0:T(8,128)(2,1)} %param.5), channel_id=1, source_target_pairs={{0,128},{128,0},{1,129},{129,1},{2,130},{130,2},{3,131},{131,3},{4... | collective-permute-start | bytes 393224 | tf_op jit(solution)/shard_map/ppermute | solution.py:19
  8.8 4.0 %collective-permute-start.2 = (s32[1,512]{1,0:T(1,128)}, s32[1,512]{1,0:T(1,128)S(1)}, u32[]{:S(2)}, u32[]{:S(2)}) collective-permute-start(s32[1,512]{1,0:T(1,128)} %param.7), channel_id=1, source_target_pairs={{0,128},{128,0},{1,129},{129,1},{2,130},{130,2},{3,131},{131,3},{4... | collective-permute-start | bytes 6152 | tf_op jit(solution)/shard_map/ppermute | solution.py:19
  8.8 3.9 %collective-permute-start.1 = (s32[1,4]{1,0:T(1,128)}, s32[1,4]{1,0:T(1,128)S(1)}, u32[]{:S(2)}, u32[]{:S(2)}) collective-permute-start(s32[1,4]{1,0:T(1,128)} %param.6), channel_id=1, source_target_pairs={{0,128},{128,0},{1,129},{129,1},{2,130},{130,2},{3,131},{131,3},{4... | collective-permute-start | bytes 56 | tf_op jit(solution)/shard_map/ppermute | solution.py:19
  14.8 35.1 %all-to-all-start = ((bf16[16,4,128,128]{3,2,1,0:T(8,128)(2,1)}), bf16[16,4,128,128]{3,2,1,0:T(8,128)(2,1)S(1)}, u32[]{:S(2)}, u32[]{:S(2)}) async-start(bf16[16,4,128,128]{3,2,1,0:T(8,128)(2,1)} %stack.3), calls=%async_computation | async-start | bytes 4194304 | tf_op jit(solution)/shard_map/all_to_all | solution.py:11
  20.6 182.0 %reduce-scatter.2.cloned.1.call-start = ((), (), s32[]{:S(2)}) async-start(), calls=%async_computation.2 | async-start | bytes 2359296 | tf_op jit(solution)/shard_map/reduce_scatter | solution.py:60
  108.9 51.6 %copy-start.1 = (s32[1,512]{1,0:T(1,128)S(1)}, s32[1,512]{1,0:T(1,128)}, u32[]{:S(2)}) copy-start(s32[1,512]{1,0:T(1,128)} %param.7) | copy-start | bytes 6148
  159.1 1.4 copy-start
Sparse Core Ops, SparseCore 0:
  160.6 41.9 reduce-scatter.1
